TPU v7x, 128 devices: a whole 4x4x4 slice. The times are simulated.
128 devices in a mesh: req: 4 (over y), exp: 32 (over z, x, core).
Axes of the slice: x: 4, y: 4, z: 4, core: 2. Of those that a mesh axis runs over, the one named last changes fastest.
Arguments:
- hidden: bfloat16 [8, 2048, 2048], P('req', 'exp'), may hold values from -6 to 6
- q_new: bfloat16 [8, 16, 2048, 128], P('req', None, 'exp'), may hold values from -480 to 480
- k_new: bfloat16 [8, 16, 2048, 128], P('req', None, 'exp'), may hold values from -6 to 6
- v_new: bfloat16 [8, 16, 2048, 128], P('req', None, 'exp'), may hold values from -6 to 6
- routes: int32 [8, 2048, 6], P('req', 'exp'), may hold values from 0 to 63, all different within a row; in each aligned block of 64 rows (0 to 63, 64 to 127, ..., all dimensions but the last counted through in order) at most 8 rows name the same one
- slot_request: int32 [8], replicated, may hold values from 0 to 7, each once
- lengths: int32 [8], replicated, may hold values from 5 to 16384, as said below
- cycle_cache: bfloat16 [128, 2, 4096, 128], P(('req', 'exp')), may hold values from -6 to 6
- sink_cache: bfloat16 [128, 2, 4, 128], P(('req', 'exp')), may hold values from -6 to 6
- w_out: bfloat16 [2048, 2048], replicated, may hold values from -0.125 to 0.125
- norm_gain: float32 [2048], replicated, may hold values from 0.5 to 1.5
- router: bfloat16 [2048, 64], replicated, may hold values from -0.125 to 0.125
- w_gate: bfloat16 [2048, 90112], P(None, ('req', 'exp')), may hold values from -0.125 to 0.125
- w_up: bfloat16 [2048, 90112], P(None, ('req', 'exp')), may hold values from -0.125 to 0.125
- w_down: bfloat16 [90112, 2048], P(('req', 'exp')), may hold values from -0.15625 to 0.15625
Outputs:
- layer_out: bfloat16 [8, 2048, 2048], P('req', 'exp')
- cycle_out: bfloat16 [128, 2, 4096, 128], P(('req', 'exp'))
Inputs may be any that keep to these rules, and one draw needn't show every extreme that they name: In every aligned block of 64 rows of routes (the rows of one request on one index of exp) no expert is named by more than 8 rows, a bound that some block reaches. `slot_request`: each request once. `lengths`: some slot has exactly 16384 cached tokens, and some other fewer than 2048.
All inputs are finite; a program needn't handle non-finite values.
Results may differ from a plain program's by a relative error of at most 0.014.
The roundings to bfloat16 on the way count: a program that leaves them out, or rounds other values in their place, can miss the bound.
Values may be sent and summed in bfloat16 or wider, within the bound.
No kernel may reach another device: no remote copies, remote signals or barrier semaphores. Data moves between devices by JAX's collectives and lax.ppermute only.
A program may use at most 192 MiB of HBM per device.

v0:
```python
import jax
import jax.numpy as jnp
from jax import lax
from jax.sharding import PartitionSpec as P

SPLIT = 2


def for_sending(array):

    def short(part):
        return part.astype(jnp.bfloat16) if part.dtype == jnp.float32 else part

    return jax.tree.map(short, array)


def rotate(vectors, positions):
    half_width = vectors.shape[-1] // 2
    frequency = 10000.0 ** (-2.0 * jnp.arange(half_width, dtype=jnp.float32) / vectors.shape[-1])
    angles = positions.astype(jnp.float32)[:, None] * frequency[None, :]
    cosine = jnp.cos(angles)
    sine_part = jnp.sin(angles)
    low_half = vectors[..., :half_width]
    high_half = vectors[..., half_width:]
    return jnp.concatenate(
        [low_half * cosine - high_half * sine_part, high_half * cosine + low_half * sine_part],
        axis=-1,
    )


def attend_block(
    q_block, row_start, cycle_from, new_upto, ordered, k_rot, value_new, sink_pair, length
):
    window = ordered.shape[1]
    score_scale = q_block.shape[1] ** (-0.5)
    key_rows = jnp.concatenate([ordered[0, cycle_from:], k_rot], 0)
    value_rows = jnp.concatenate([ordered[1, cycle_from:], value_new], 0)
    row_ids = row_start + jnp.arange(q_block.shape[0], dtype=jnp.int32)
    cycle_cols = cycle_from + jnp.arange(window - cycle_from, dtype=jnp.int32)
    cycle_visible = (cycle_cols[None, :] > row_ids[:, None]) & (
        cycle_cols[None, :] >= window - length
    )
    new_visible = jnp.arange(new_upto, dtype=jnp.int32)[None, :] <= row_ids[:, None]
    visible = jnp.concatenate([cycle_visible, new_visible], 1)
    scores = (
        jnp.einsum("qd,kd->qk", q_block, key_rows, preferred_element_type=jnp.float32) * score_scale
    )
    scores = jnp.where(visible, scores, -jnp.inf)
    sink_scores = (
        jnp.einsum("qd,kd->qk", q_block, sink_pair[0], preferred_element_type=jnp.float32)
        * score_scale
    )
    sink_visible = (
        jnp.arange(sink_pair.shape[1], dtype=jnp.int32)[None, :]
        <= (length + row_ids - window)[:, None]
    )
    sink_scores = jnp.where(sink_visible, sink_scores, -jnp.inf)
    highest = jnp.maximum(jnp.max(scores, axis=1), jnp.max(sink_scores, axis=1))[:, None]
    weights = jnp.exp(scores - highest)
    sink_weights = jnp.exp(sink_scores - highest)
    denominator = jnp.sum(weights, axis=1) + jnp.sum(sink_weights, axis=1)
    blended = jnp.dot(weights.astype(jnp.bfloat16), value_rows, preferred_element_type=jnp.float32)
    blended = blended + jnp.dot(
        sink_weights.astype(jnp.bfloat16), sink_pair[1], preferred_element_type=jnp.float32
    )
    return (blended / denominator[:, None]).astype(jnp.bfloat16)


def attend_pair(query_rows, key_new, value_new, cycle_pair, sink_pair, length):
    seq_len = query_rows.shape[0]
    window = cycle_pair.shape[1]
    block_rows = min(512, seq_len)
    positions = length + jnp.arange(seq_len, dtype=jnp.int32)
    q_rot = rotate(query_rows.astype(jnp.float32), positions).astype(jnp.bfloat16)
    k_rot = rotate(key_new.astype(jnp.float32), positions).astype(jnp.bfloat16)
    ordered = jnp.roll(cycle_pair, -(length % window), axis=1)
    outputs = []
    for block_number in range(seq_len // block_rows):
        row_start = block_number * block_rows
        cycle_from = 0
        outputs.append(
            attend_block(
                q_rot[row_start : row_start + block_rows],
                row_start,
                cycle_from,
                seq_len,
                ordered,
                k_rot,
                value_new,
                sink_pair,
                length,
            )
        )
    context = jnp.concatenate(outputs, 0)
    retained = ordered[:, seq_len:]
    appended = jnp.stack([k_rot, value_new])
    updated = jnp.roll(
        jnp.concatenate([retained, appended], 1), (length + seq_len) % window, axis=1
    )
    return (context, updated)


def on_device(
    hidden,
    q_new,
    k_new,
    v_new,
    routes,
    slot_request,
    lengths,
    cycle_cache,
    sink_cache,
    w_out,
    norm_gain,
    router,
    w_gate,
    w_up,
    w_down,
):
    group_width = lax.axis_size("exp")
    group_count = lax.axis_size("req")
    devices_all = group_count * group_width
    group_index = lax.axis_index("req")
    member_index = lax.axis_index("exp")
    slots_here, local_rows, model_width = hidden.shape
    head_count = q_new.shape[1]
    head_dim = q_new.shape[3]
    experts_all = router.shape[1]
    arrived = (
        lax.all_gather(hidden, "req", axis=0, tiled=True),
        lax.all_gather(q_new, "req", axis=0, tiled=True),
        lax.all_gather(k_new, "req", axis=0, tiled=True),
        lax.all_gather(v_new, "req", axis=0, tiled=True),
        lax.all_gather(routes, "req", axis=0, tiled=True),
    )
    requests = lax.dynamic_slice_in_dim(slot_request, group_index * slots_here, slots_here)
    hidden_sel, query_sel, key_sel, value_sel, route_sel = [
        jnp.take(arrival, requests, axis=0) for arrival in arrived
    ]
    pair_count = slots_here * head_count
    query_pairs, key_pairs, value_pairs = (
        lax.all_to_all(
            query_sel.reshape(pair_count, local_rows, head_dim),
            "exp",
            split_axis=0,
            concat_axis=1,
            tiled=True,
        ),
        lax.all_to_all(
            key_sel.reshape(pair_count, local_rows, head_dim),
            "exp",
            split_axis=0,
            concat_axis=1,
            tiled=True,
        ),
        lax.all_to_all(
            value_sel.reshape(pair_count, local_rows, head_dim),
            "exp",
            split_axis=0,
            concat_axis=1,
            tiled=True,
        ),
    )
    pairs_here = pair_count // group_width
    pair_ids = member_index * pairs_here + jnp.arange(pairs_here, dtype=jnp.int32)
    pair_lengths = jnp.take(lengths, group_index * slots_here + pair_ids // head_count)
    context, cycle_out = lax.map(
        lambda packed: attend_pair(*packed),
        (query_pairs, key_pairs, value_pairs, cycle_cache, sink_cache, pair_lengths),
    )
    context_rows = jax.tree.map(
        lambda part, own: part.astype(own.dtype),
        lax.all_to_all(for_sending(context), "exp", split_axis=1, concat_axis=0, tiled=True),
        context,
    ).reshape(slots_here, head_count, local_rows, head_dim)
    projected = jnp.einsum(
        "shqd,hde->sqe",
        context_rows,
        w_out.reshape(head_count, head_dim, model_width),
        preferred_element_type=jnp.float32,
    )
    residual = hidden_sel.astype(jnp.float32) + projected
    inverse = lax.rsqrt(jnp.mean(residual * residual, axis=-1, keepdims=True) + 1e-06)
    normed = (residual * inverse * norm_gain).astype(jnp.bfloat16)
    logits = jnp.einsum("sqd,de->sqe", normed, router, preferred_element_type=jnp.float32)
    gates = jax.nn.softmax(jnp.take_along_axis(logits, route_sel, axis=2), axis=-1)
    most_slots = max(2, local_rows // 8)
    expert_ids = jnp.arange(experts_all, dtype=jnp.int32)
    per_row = jnp.any(route_sel[..., None] == expert_ids, axis=2).astype(jnp.int32)
    earlier = jnp.cumsum(per_row, axis=1) - per_row
    ranks = jnp.take_along_axis(earlier, route_sel, axis=2)
    slot_ids = jnp.broadcast_to(
        jnp.arange(slots_here, dtype=jnp.int32)[:, None, None], route_sel.shape
    )
    spread = jnp.broadcast_to(normed[:, :, None, :], route_sel.shape + (model_width,))
    buffer = (
        jnp.zeros((experts_all, slots_here, most_slots, model_width), jnp.bfloat16)
        .at[route_sel, slot_ids, ranks]
        .set(spread)
    )
    sub_here = experts_all * SPLIT // devices_all
    piece_shape = (devices_all, sub_here, slots_here, most_slots, model_width)
    half_units = w_gate.shape[1] // sub_here
    gate_local = w_gate.reshape(model_width, sub_here, half_units)
    up_local = w_up.reshape(model_width, sub_here, half_units)
    down_local = w_down.reshape(sub_here, half_units, model_width)
    outgoing = jnp.broadcast_to(
        buffer[:, None], (experts_all, SPLIT, slots_here, most_slots, model_width)
    ).reshape(piece_shape)
    received = lax.all_to_all(outgoing, ("req", "exp"), split_axis=0, concat_axis=0, tiled=True)
    gate_part = jnp.einsum(
        "nsrkd,dsf->nsrkf", received, gate_local, preferred_element_type=jnp.float32
    )
    up_part = jnp.einsum("nsrkd,dsf->nsrkf", received, up_local, preferred_element_type=jnp.float32)
    active = (jax.nn.silu(gate_part) * up_part).astype(jnp.bfloat16)
    returned = lax.all_to_all(
        jnp.einsum(
            "nsrkf,sfd->nsrkd", active, down_local, preferred_element_type=jnp.float32
        ).astype(jnp.bfloat16),
        ("req", "exp"),
        split_axis=0,
        concat_axis=0,
        tiled=True,
    )
    pieces = returned.reshape(experts_all, SPLIT, slots_here, most_slots, model_width).astype(
        jnp.float32
    )
    summed = jnp.sum(pieces, axis=1)
    picked = summed[route_sel, slot_ids, ranks]
    moe = jnp.sum(gates[..., None] * picked, axis=2)
    layer_out = (residual + moe).astype(jnp.bfloat16)
    return (layer_out, cycle_out)


def solution(mesh):
    in_specs = (
        P("req", "exp", None),
        P("req", None, "exp", None),
        P("req", None, "exp", None),
        P("req", None, "exp", None),
        P("req", "exp", None),
        P(),
        P(),
        P(("req", "exp"), None, None, None),
        P(("req", "exp"), None, None, None),
        P(),
        P(),
        P(),
        P(None, ("req", "exp")),
        P(None, ("req", "exp")),
        P(("req", "exp"), None),
    )
    out_specs = (P("req", "exp", None), P(("req", "exp"), None, None, None))
    return jax.shard_map(
        on_device, mesh=mesh, in_specs=in_specs, out_specs=out_specs, check_vma=False
    )
```

profile of v0, /device:TPU:10, one launch (start us, length us, event | category | flops | bytes accessed | tf_op | source)
XLA Modules:
  0.0 760.2 jit_solution(11624940726540011022)
XLA Ops:
  14.7 12.3 %all_gather.19 = s32[8,64,6]{1,2,0:T(8,128)S(1)} all-gather(s32[2,64,6]{1,2,0:T(8,128)S(1)} %copy.55), channel_id=1, replica_groups=mesh['req'=4,'exp'=32] {'req'}, dimensions={0}, use_global_device_ids=true | all-gather | bytes 15360 | tf_op jit(solution)/shard_map/all_gather | solution.py:134
  37.7 8.3 %fusion.13 = (pred[512,4096]{1,0:T(32,128)(4,1)}, pred[512,4096]{1,0:T(32,128)(4,1)}, pred[512,4096]{1,0:T(32,128)(4,1)}, pred[512,4096]{1,0:T(32,128)(4,1)}) fusion(pred[4096]{0:T(1024)(128)(4,1)S(1)} %iota_compare_fusion.9, s32[512]{0:T(512)S(1)} %iota_add_fusion.2, s32[512]{0:T(512)S(1)} %get-tuple-element.90, s32[512]{0:T(512)S(1)} %get-tuple-element.89), kind=kLoop, calls=%fused_computation.37 | loop fusion | flops 16777216 | bytes 8398848 | tf_op jit(solution)/shard_map/while/body/eval_jaxpr/and | solution.py:40
  48.2 26.1 %all-gather.9.cloned.1.call-done = bf16[8,16,64,128]{3,2,1,0:T(8,128)(2,1)} async-done(((bf16[2,16,64,128]{3,2,1,0:T(8,128)(2,1)}), bf16[8,16,64,128]{3,2,1,0:T(8,128)(2,1)}) %all-gather.9.cloned.1.call-update) | async-done | bytes 2097168 | tf_op jit(solution)/shard_map/all_gather | solution.py:132
  77.3 29.5 %all-gather.7.cloned.1.call-done = bf16[8,16,64,128]{3,2,1,0:T(8,128)(2,1)} async-done(((bf16[2,16,64,128]{3,2,1,0:T(8,128)(2,1)}), bf16[8,16,64,128]{3,2,1,0:T(8,128)(2,1)}) %all-gather.7.cloned.1.call-update) | async-done | bytes 2097168 | tf_op jit(solution)/shard_map/all_gather | solution.py:131
  112.3 7.6 all-to-all-start.1
  121.5 8.7 %all-to-all-done.1 = bf16[32,64,128]{2,1,0:T(8,128)(2,1)S(1)} async-done(((bf16[32,64,128]{2,1,0:T(8,128)(2,1)}), bf16[32,64,128]{2,1,0:T(8,128)(2,1)S(1)}, u32[]{:S(2)}, u32[]{:S(2)}) %all-to-all-start.1) | async-done | bytes 524320 | tf_op jit(solution)/shard_map/all_to_all | solution.py:149
  130.2 5.7 all-to-all-start
  137.0 9.4 %all-to-all-done = bf16[32,64,128]{2,1,0:T(8,128)(2,1)} async-done(((bf16[32,64,128]{2,1,0:T(8,128)(2,1)}), bf16[32,64,128]{2,1,0:T(8,128)(2,1)}, u32[]{:S(2)}, u32[]{:S(2)}) %all-to-all-start) | async-done | bytes 524320 | tf_op jit(solution)/shard_map/all_to_all | solution.py:142
  152.6 7.5 fusion.78
  171.0 7.5 fusion.19
  186.9 8.4 %fusion.143 = (f32[512]{0:T(512)S(1)}, f32[512,6144]{1,0:T(8,128)S(1)}) fusion(bf16[512,128]{1,0:T(8,128)(2,1)S(1)} %copy-done.21, bf16[2048,64]{1,0:T(8,128)(2,1)} %copy-done.12, bf16[2048,64]{1,0:T(8,128)(2,1)S(1)} %copy-done.11, bf16[4096,128]{1,0:T(8,128)(2,1)} %get-tuple-element.45, pred[512,2048]{1,0:T(32,128)(4,1)} %iota_compare_fusion.6, ...), kind=kOutput, calls=%fused_computation.234 | convolution fusion | flops 822607360 | bytes 17434624 | tf_op jit(solution)/shard_map/while/body/eval_jaxpr/qd,kd->qk/dot_general | solution.py:46
  197.4 8.6 %fusion.145 = (f32[512]{0:T(512)S(1)}, f32[512,6144]{1,0:T(8,128)}) fusion(bf16[512,128]{1,0:T(8,128)(2,1)S(1)} %copy-done.20, bf16[2048,64]{1,0:T(8,128)(2,1)} %copy-done.12, bf16[2048,64]{1,0:T(8,128)(2,1)S(1)} %copy-done.11, bf16[4096,128]{1,0:T(8,128)(2,1)} %get-tuple-element.45, pred[512,2048]{1,0:T(32,128)(4,1)} %iota_compare_fusion.7, ...), kind=kOutput, calls=%fused_computation.236 | convolution fusion | flops 822607360 | bytes 17434624 | tf_op jit(solution)/shard_map/while/body/eval_jaxpr/qd,kd->qk/dot_general | solution.py:46
  206.1 6.4 fusion.1
  220.0 8.9 %copy.87 = bf16[1,2048,128]{2,0,1:T(2,128)(2,1)} copy(bf16[1,2048,128]{2,1,0:T(8,128)(2,1)S(1)} %maximum_bitcast_fusion) | data formatting | bytes 1048576 | tf_op jit(solution)/shard_map/while/body/jit(dynamic_update_index_in_dim)/broadcast_in_dim | solution.py:167
  229.4 13.7 %reduce = bf16[2048,128]{1,0:T(8,128)(2,1)} reduce(bf16[2048,1,128]{2,1,0:T(2,128)(2,1)} %bitcast.188, bf16[]{:T(256)} %broadcast.485), dimensions={1}, to_apply=%bitcast.178.reduce_sub_computation | reduce | bytes 1048578
  245.1 7.5 all-to-all-start.3
  255.3 6.6 gather_fusion.4
  280.9 6.3 reshape.375
  289.7 143.6 %scatter_fusion = bf16[64,2,8,2048]{3,2,1,0:T(8,128)(2,1)} fusion(bf16[64,2,8,2048]{3,2,1,0:T(8,128)(2,1)} %broadcast_in_dim.180, s32[768]{0:T(1024)S(1)} %reshape.373, bf16[768,2048]{1,0:T(8,128)(2,1)} %reshape.375), kind=kCustom, calls=%fused_computation.8 | custom fusion | bytes 9446400 | tf_op jit(solution)/shard_map/scatter | solution.py:199
  433.3 6.8 broadcast_in_dim.183
  440.1 106.9 %all_to_all.49 = bf16[128,1,2,8,2048]{4,3,2,1,0:T(8,128)(2,1)S(1)} all-to-all(bf16[128,1,2,8,2048]{4,3,2,1,0:T(8,128)(2,1)} %bitcast.180), channel_id=1, replica_groups=mesh['req'=4,'exp'=32] {'req','exp'}, dimensions={0} | all-to-all | bytes 16777216 | tf_op jit(solution)/shard_map/all_to_all | solution.py:210
  550.2 12.8 %fusion.9 = f32[128,2,8,704]{0,3,2,1:T(8,128)} fusion(bf16[128,1,2,8,2048]{4,3,2,1,0:T(8,128)(2,1)S(1)} %all_to_all.49, bf16[2048,704]{0,1:T(8,128)(2,1)S(1)} %copy-done.34), kind=kOutput, calls=%fused_computation.27 | convolution fusion | flops 5905580032 | bytes 17039360 | tf_op jit(solution)/shard_map/nsrkd,dsf->nsrkf/dot_general | solution.py:214
  563.0 27.3 %convert_bitcast_fusion = bf16[128,1,2,8,2048]{4,0,3,2,1:T(8,128)(2,1)} fusion(bf16[704,2048]{1,0:T(8,128)(2,1)S(1)} %copy-done, f32[128,2,8,704]{0,3,2,1:T(8,128)} %fusion.9, bf16[128,1,2,8,2048]{4,3,2,1,0:T(8,128)(2,1)} %copy-done.7, bf16[2048,704]{0,1:T(8,128)(2,1)} %param.31), kind=kOutput, calls=%fused_computation.32 | convolution fusion | flops 11824005120 | bytes 28311552 | tf_op jit(solution)/shard_map/nsrkf,sfd->nsrkd/dot_general | solution.py:217
  590.3 11.2 %copy.62 = bf16[128,1,2,8,2048]{4,3,2,1,0:T(8,128)(2,1)} copy(bf16[128,1,2,8,2048]{4,0,3,2,1:T(8,128)(2,1)} %convert_bitcast_fusion) | data formatting | bytes 16777216 | tf_op jit(solution)/shard_map/convert_element_type | solution.py:219
  601.6 6.3 all-to-all-start.5
  610.5 8.7 %fusion.44 = bf16[1,2,4096,128]{3,2,1,0:T(8,128)(2,1)} fusion(s32[]{:T(128)S(6)} %select_n.213, bf16[2,2048,128]{2,1,0:T(8,128)(2,1)} %slice.118, bf16[1,2048,64]{2,1,0:T(8,128)(2,1)} %bitcast.190, bf16[1,2048,64]{2,1,0:T(8,128)(2,1)} %bitcast.191, bf16[1,2048,128]{2,1,0:T(8,128)(2,1)S(1)} %bitcast.185), kind=kLoop, calls=%fused_computation.80 | loop fusion | flops 16777216 | bytes 4194308 | tf_op jit(solution)/shard_map/while/body/jit(dynamic_update_index_in_dim)/broadcast_in_dim | solution.py:167
  619.4 6.6 gather_fusion.3
  626.4 85.9 %all-to-all-done.5 = bf16[128,1,2,8,2048]{4,3,2,1,0:T(8,128)(2,1)} async-done(((bf16[128,1,2,8,2048]{4,3,2,1,0:T(8,128)(2,1)}), bf16[128,1,2,8,2048]{4,3,2,1,0:T(8,128)(2,1)}, u32[]{:S(2)}, u32[]{:S(2)}) %all-to-all-start.5) | async-done | bytes 8388640 | tf_op jit(solution)/shard_map/all_to_all | solution.py:216
  712.4 9.6 %convert_reduce_fusion = f32[64,2,8,2048]{3,2,1,0:T(8,128)} fusion(bf16[64,2,2,8,2048]{4,3,2,1,0:T(8,128)(2,1)} %bitcast.179), kind=kLoop, calls=%fused_computation.10 | loop fusion | flops 6291456 | bytes 16777216 | tf_op jit(solution)/shard_map/reduce_sum | solution.py:228
  722.0 15.5 %gather_fusion.2 = f32[768,2048]{1,0:T(8,128)} fusion(f32[64,2,8,2048]{3,2,1,0:T(8,128)} %convert_reduce_fusion, s32[768]{0:T(1024)S(1)} %reshape.355), kind=kCustom, calls=%fused_computation.5 | custom fusion | bytes 12592128 | tf_op jit(solution)/shard_map/gather | solution.py:229
  737.5 8.1 %reshape.358 = f32[2,64,6,2048]{3,2,1,0:T(8,128)} reshape(f32[768,2048]{1,0:T(8,128)} %gather_fusion.2) | data formatting | bytes 12582912 | tf_op jit(solution)/shard_map/gather | solution.py:229
  745.6 6.7 multiply_reduce_fusion
  (170 shorter events, 99.4 us)
Async XLA Ops:
  7.2 555.9 %copy-start = (bf16[704,2048]{1,0:T(8,128)(2,1)S(1)}, bf16[704,2048]{1,0:T(8,128)(2,1)}, u32[]{:S(2)}) copy-start(bf16[704,2048]{1,0:T(8,128)(2,1)} %param.33) | copy-start | bytes 8650756
  7.2 38.8 %all-gather.11.cloned.1.call-start = ((), (), s32[]{:S(2)}) async-start(), calls=%async_computation.9 | async-start | bytes 2621440 | tf_op jit(solution)/shard_map/all_gather | solution.py:133
  7.9 66.4 %all-gather.9.cloned.1.call-start = ((), (), s32[]{:S(2)}) async-start(), calls=%async_computation.8 | async-start | bytes 2621440 | tf_op jit(solution)/shard_map/all_gather | solution.py:132
  8.7 98.1 %all-gather.7.cloned.1.call-start = ((), (), s32[]{:S(2)}) async-start(), calls=%async_computation.7 | async-start | bytes 2621440 | tf_op jit(solution)/shard_map/all_gather | solution.py:131
  9.4 253.0 %all-gather.5.cloned.1.call-start = ((), (), s32[]{:S(2)}) async-start(), calls=%async_computation.6 | async-start | bytes 2621440 | tf_op jit(solution)/shard_map/all_gather | solution.py:130
  14.0 95.8 %copy-start.29 = (pred[2]{0:T(512)(128)(4,1)}, pred[2]{0:T(512)(128)(4,1)S(1)}, u32[]{:S(2)}) copy-start(pred[2]{0:T(512)(128)(4,1)S(1)} %get-tuple-element.42) | copy-start | bytes 10
  14.0 92.8 %copy-start.31 = (s32[1024]{0:T(1024)}, s32[1024]{0:T(1024)S(1)}, u32[]{:S(2)}) copy-start(s32[1024]{0:T(1024)S(1)} %pad_clamp_fusion) | copy-start | bytes 12292
  27.6 225.1 %copy-start.27 = (s32[2,64,6]{1,2,0:T(8,128)}, s32[2,64,6]{1,2,0:T(8,128)S(1)}, u32[]{:S(2)}) copy-start(s32[2,64,6]{1,2,0:T(8,128)S(1)} %broadcast_select_fusion.3) | copy-start | bytes 9220
  112.3 17.9 %all-to-all-start.1 = ((bf16[32,64,128]{2,1,0:T(8,128)(2,1)}), bf16[32,64,128]{2,1,0:T(8,128)(2,1)S(1)}, u32[]{:S(2)}, u32[]{:S(2)}) async-start(bf16[32,64,128]{2,1,0:T(8,128)(2,1)} %bitcast.195), calls=%async_computation.1 | async-start | bytes 1048576 | tf_op jit(solution)/shard_map/all_to_all | solution.py:149
  130.2 16.2 %all-to-all-start = ((bf16[32,64,128]{2,1,0:T(8,128)(2,1)}), bf16[32,64,128]{2,1,0:T(8,128)(2,1)}, u32[]{:S(2)}, u32[]{:S(2)}) async-start(bf16[32,64,128]{2,1,0:T(8,128)(2,1)} %bitcast.194), calls=%async_computation | async-start | bytes 1048576 | tf_op jit(solution)/shard_map/all_to_all | solution.py:142
  146.4 24.5 %all-to-all-start.2 = ((bf16[32,64,128]{2,1,0:T(8,128)(2,1)}), bf16[32,64,128]{2,1,0:T(8,128)(2,1)S(1)}, u32[]{:S(2)}, u32[]{:S(2)}) async-start(bf16[32,64,128]{2,1,0:T(8,128)(2,1)} %bitcast.193), calls=%async_computation.2 | async-start | bytes 1048576 | tf_op jit(solution)/shard_map/all_to_all | solution.py:156
  152.5 8.7 %copy-start.33 = (bf16[1,2,4,128]{3,2,1,0:T(4,128)(2,1)S(1)}, bf16[1,2,4,128]{3,2,1,0:T(4,128)(2,1)}, u32[]{:S(2)}) copy-start(bf16[1,2,4,128]{3,2,1,0:T(4,128)(2,1)} %param.27) | copy-start | bytes 6148
  152.5 8.9 %copy-start.15 = (pred[512,4096]{1,0:T(32,128)(4,1)S(1)}, pred[512,4096]{1,0:T(32,128)(4,1)}, u32[]{:S(2)}) copy-start(pred[512,4096]{1,0:T(32,128)(4,1)} %get-tuple-element.61) | copy-start | bytes 6291460
  152.6 8.9 %copy-start.17 = (pred[512,2048]{1,0:T(32,128)(4,1)S(1)}, pred[512,2048]{1,0:T(32,128)(4,1)}, u32[]{:S(2)}) copy-start(pred[512,2048]{1,0:T(32,128)(4,1)} %iota_compare_fusion.4) | copy-start | bytes 3145732
  152.6 8.9 %copy-start.18 = (bf16[4096,128]{1,0:T(8,128)(2,1)S(1)}, bf16[4096,128]{1,0:T(8,128)(2,1)}, u32[]{:S(2)}) copy-start(bf16[4096,128]{1,0:T(8,128)(2,1)} %get-tuple-element.45) | copy-start | bytes 3145732
  170.9 7.6 copy-start.22
  170.9 7.7 %copy-start.11 = (bf16[2048,64]{1,0:T(8,128)(2,1)S(1)}, bf16[2048,64]{1,0:T(8,128)(2,1)}, u32[]{:S(2)}) copy-start(bf16[2048,64]{1,0:T(8,128)(2,1)} %copy-done.10) | copy-start | bytes 786436
  171.0 7.7 %copy-start.13 = (bf16[2048,64]{1,0:T(8,128)(2,1)S(1)}, bf16[2048,64]{1,0:T(8,128)(2,1)}, u32[]{:S(2)}) copy-start(bf16[2048,64]{1,0:T(8,128)(2,1)} %copy-done.12) | copy-start | bytes 786436
  171.0 7.7 %copy-start.14 = (pred[512,4096]{1,0:T(32,128)(4,1)S(1)}, pred[512,4096]{1,0:T(32,128)(4,1)}, u32[]{:S(2)}) copy-start(pred[512,4096]{1,0:T(32,128)(4,1)} %get-tuple-element.60) | copy-start | bytes 6291460
  171.0 7.7 %copy-start.16 = (pred[512,2048]{1,0:T(32,128)(4,1)S(1)}, pred[512,2048]{1,0:T(32,128)(4,1)}, u32[]{:S(2)}) copy-start(pred[512,2048]{1,0:T(32,128)(4,1)} %iota_compare_fusion.5) | copy-start | bytes 3145732
  171.0 7.7 %copy-start.19 = (bf16[4096,128]{1,0:T(8,128)(2,1)S(1)}, bf16[4096,128]{1,0:T(8,128)(2,1)}, u32[]{:S(2)}) copy-start(bf16[4096,128]{1,0:T(8,128)(2,1)} %get-tuple-element.45) | copy-start | bytes 3145732
  206.1 6.5 copy-start.23
  206.1 6.8 copy-start.24
  245.1 20.4 %all-to-all-start.3 = ((bf16[32,2,4096]{2,1,0:T(2,128)(2,1)}), bf16[32,2,4096]{2,1,0:T(2,128)(2,1)}, u32[]{:S(2)}, u32[]{:S(2)}) async-start(bf16[32,2,4096]{2,1,0:T(2,128)(2,1)} %reshape.397), calls=%async_computation.3 | async-start | bytes 1048576 | tf_op jit(solution)/shard_map/all_to_all | solution.py:173
  255.3 6.8 copy-start.30
  271.3 6.1 copy-start.32
  440.1 110.1 %copy-start.34 = (bf16[2048,704]{0,1:T(8,128)(2,1)S(1)}, bf16[2048,704]{0,1:T(8,128)(2,1)}, u32[]{:S(2)}) copy-start(bf16[2048,704]{0,1:T(8,128)(2,1)} %param.32) | copy-start | bytes 8650756
  601.6 110.8 %all-to-all-start.5 = ((bf16[128,1,2,8,2048]{4,3,2,1,0:T(8,128)(2,1)}), bf16[128,1,2,8,2048]{4,3,2,1,0:T(8,128)(2,1)}, u32[]{:S(2)}, u32[]{:S(2)}) async-start(bf16[128,1,2,8,2048]{4,3,2,1,0:T(8,128)(2,1)} %copy.62), calls=%async_computation.5 | async-start | bytes 16777216 | tf_op jit(solution)/shard_map/all_to_all | solution.py:216
  610.4 8.7 %copy-start.9 = (bf16[2,64,2048]{2,1,0:T(8,128)(2,1)S(1)}, bf16[2,64,2048]{2,1,0:T(8,128)(2,1)}, u32[]{:S(2)}) copy-start(bf16[2,64,2048]{2,1,0:T(8,128)(2,1)} %copy-done.8) | copy-start | bytes 1572868
  610.4 8.7 %copy-start.25 = (bf16[2048,64]{0,1:T(8,128)(2,1)S(1)}, bf16[2048,64]{0,1:T(8,128)(2,1)}, u32[]{:S(2)}) copy-start(bf16[2048,64]{0,1:T(8,128)(2,1)} %param.30) | copy-start | bytes 786436
  619.4 6.8 copy-start.28
  745.6 6.7 copy-start.6
  (12 other events, 32.3 us)
Sparse Core Ops, SparseCore 0:
  9.6 32.1 all-gather.10
  43.5 30.7 all-gather.8
  76.0 30.7 all-gather.6
  108.3 30.7 all-gather.4
where the time goes:
time: 772 us; the launch traced here: 760 us
  local copies, waits for them, and re-layouts  261 us (34%)
  waiting for transfers between devices  162 us (21%)
  blocking collectives  119 us (15%)
  other arithmetic  86.2 us (11%)
  matrix products  84.1 us (11%)
  starting transfers between devices  32.2 us (4%)
  between operations  15.8 us (2%)
    scatter x1, local copies, waits for them, and re-layouts, on_device(): buffer = jnp.zeros((experts_all, slots_here, most_slots, model_width), jn...  144 us
    all_to_all x1, blocking collectives, on_device(): lax.all_to_all(outgoing, ('req', 'exp'), split_axis=0, concat_axis=0, til...  107 us
    all_to_all x1, waiting for transfers between devices, on_device(): lax.all_to_all(jnp.einsum('nsrkf,sfd->nsrkd', active, down_local, preferr...  85.9 us
    all_gather x1, waiting for transfers between devices, on_device(): lax.all_gather(q_new, 'req', axis=0, tiled=True)  29.5 us
    dot_general x1, matrix products, on_device(): jnp.einsum('nsrkf,sfd->nsrkd', active, down_local, preferred_element_type...  27.3 us
    all_gather x1, waiting for transfers between devices, on_device(): lax.all_gather(k_new, 'req', axis=0, tiled=True)  26.1 us
    gather x2, local copies, waits for them, and re-layouts, on_device(): picked = summed[route_sel, slot_ids, ranks]  23.6 us
    dot_general x4, matrix products, attend_block(): jnp.einsum('qd,kd->qk', q_block, key_rows, preferred_element_type=jnp.flo...  23.1 us
  transfers between devices with their start and end apart: 9, of which 5 were waited for; matrix products, arithmetic and copies ran while one was open for 20% of the time, Pallas kernels for 0%

commit v1 on v0

--- a/solution.py
+++ b/solution.py
@@ -1,9 +1,25 @@
+import functools
 import jax
 import jax.numpy as jnp
 from jax import lax
 from jax.sharding import PartitionSpec as P
 
 SPLIT = 2
+
+
+def _produce_chains(piece_in, bus_axis):
+    n_chips = lax.psum(1, axis_name=bus_axis)
+    far_arr = lax.all_to_all(
+        jnp.tile(piece_in, [n_chips if j0 == 0 else 1 for j0 in range(piece_in.ndim)]),
+        axis_name=bus_axis,
+        split_axis=0,
+        concat_axis=0,
+        tiled=True,
+    )
+    return far_arr
+
+
+sectors_draw = functools.partial(_produce_chains, bus_axis="req")
 
 
 def for_sending(array):
@@ -128,7 +144,7 @@
     experts_all = router.shape[1]
     arrived = (
         lax.all_gather(hidden, "req", axis=0, tiled=True),
-        lax.all_gather(q_new, "req", axis=0, tiled=True),
+        sectors_draw(q_new),
         lax.all_gather(k_new, "req", axis=0, tiled=True),
         lax.all_gather(v_new, "req", axis=0, tiled=True),
         lax.all_gather(routes, "req", axis=0, tiled=True),

time: 772 us -> 756 us (0.979)
  waiting for transfers between devices: 162 us -> 109 us
  blocking collectives: 119 us -> 151 us
    all_gather x1, blocking collectives: 12.3 us -> 43.9 us  [on_device(): lax.all_gather(routes, 'req', axis=0, tiled=True)]
    all_gather x1 -> x0, waiting for transfers between devices: 29.5 us -> none  [on_device(): lax.all_gather(q_new, 'req', axis=0, tiled=True)]
    all_gather x1, waiting for transfers between devices: 26.1 us -> 2.94 us  [on_device(): lax.all_gather(k_new, 'req', axis=0, tiled=True)]
    unnamed x75 -> x81, local copies, waits for them, and re-layouts: 23 us -> 22.3 us
  transfers between devices with their start and end apart: 9 -> 9, of which waited for: 5 -> 4; matrix products, arithmetic and copies ran while one was open for 20% -> 21% of each run, Pallas kernels for 0% -> 0%
where the time goes in v1:
time: 756 us; the launch traced here: 744 us
  local copies, waits for them, and re-layouts  262 us (35%)
  blocking collectives  151 us (20%)
  waiting for transfers between devices  109 us (14%)
  other arithmetic  85.4 us (11%)
  matrix products  84.1 us (11%)
  starting transfers between devices  37 us (5%)
  between operations  15.8 us (2%)
    scatter x1, local copies, waits for them, and re-layouts, on_device(): buffer = jnp.zeros((experts_all, slots_here, most_slots, model_width), jn...  144 us
    all_to_all x1, blocking collectives, on_device(): lax.all_to_all(outgoing, ('req', 'exp'), split_axis=0, concat_axis=0, til...  107 us
    all_to_all x1, waiting for transfers between devices, on_device(): lax.all_to_all(jnp.einsum('nsrkf,sfd->nsrkd', active, down_local, preferr...  85.9 us
    all_gather x1, blocking collectives, on_device(): lax.all_gather(routes, 'req', axis=0, tiled=True)  43.9 us
    dot_general x1, matrix products, on_device(): jnp.einsum('nsrkf,sfd->nsrkd', active, down_local, preferred_element_type...  27.3 us
    gather x2, local copies, waits for them, and re-layouts, on_device(): picked = summed[route_sel, slot_ids, ranks]  23.6 us
    dot_general x4, matrix products, attend_block(): jnp.einsum('qd,kd->qk', q_block, key_rows, preferred_element_type=jnp.flo...  23.1 us
    unnamed x81, local copies, waits for them, and re-layouts  22.3 us
  transfers between devices with their start and end apart: 9, of which 4 were waited for; matrix products, arithmetic and copies ran while one was open for 21% of the time, Pallas kernels for 0%

profile of v1, /device:TPU:10, one launch (start us, length us, event | category | flops | bytes accessed | tf_op | source)
XLA Modules:
  0.0 744.2 jit_solution(15395177708270646481)
XLA Ops:
  20.0 43.9 %all_gather.15 = s32[8,64,6]{1,2,0:T(8,128)S(1)} all-gather(s32[2,64,6]{1,2,0:T(8,128)S(1)} %copy.55), channel_id=1, replica_groups=mesh['req'=4,'exp'=32] {'req'}, dimensions={0}, use_global_device_ids=true | all-gather | bytes 15360 | tf_op jit(solution)/shard_map/all_gather | solution.py:150
  74.5 8.4 %fusion.13 = (pred[512,4096]{1,0:T(32,128)(4,1)}, pred[512,4096]{1,0:T(32,128)(4,1)}, pred[512,4096]{1,0:T(32,128)(4,1)}, pred[512,4096]{1,0:T(32,128)(4,1)}) fusion(pred[4096]{0:T(1024)(128)(4,1)S(1)} %iota_compare_fusion.9, s32[512]{0:T(512)S(1)} %iota_add_fusion.2, s32[512]{0:T(512)S(1)} %get-tuple-element.90, s32[512]{0:T(512)S(1)} %get-tuple-element.89), kind=kLoop, calls=%fused_computation.37 | loop fusion | flops 16777216 | bytes 8398848 | tf_op jit(solution)/shard_map/while/body/eval_jaxpr/and | solution.py:56
  96.5 7.6 %all-to-all-start.2 = ((bf16[32,64,128]{2,1,0:T(8,128)(2,1)}), bf16[32,64,128]{2,1,0:T(8,128)(2,1)S(1)}, u32[]{:S(2)}, u32[]{:S(2)}) async-start(bf16[32,64,128]{2,1,0:T(8,128)(2,1)} %bitcast.197), calls=%async_computation.2 | async-start | bytes 1048576 | tf_op jit(solution)/shard_map/all_to_all | solution.py:165
  105.7 8.7 %all-to-all-done.2 = bf16[32,64,128]{2,1,0:T(8,128)(2,1)S(1)} async-done(((bf16[32,64,128]{2,1,0:T(8,128)(2,1)}), bf16[32,64,128]{2,1,0:T(8,128)(2,1)S(1)}, u32[]{:S(2)}, u32[]{:S(2)}) %all-to-all-start.2) | async-done | bytes 524320 | tf_op jit(solution)/shard_map/all_to_all | solution.py:165
  114.5 5.7 all-to-all-start.1
  121.2 9.4 %all-to-all-done.1 = bf16[32,64,128]{2,1,0:T(8,128)(2,1)} async-done(((bf16[32,64,128]{2,1,0:T(8,128)(2,1)}), bf16[32,64,128]{2,1,0:T(8,128)(2,1)}, u32[]{:S(2)}, u32[]{:S(2)}) %all-to-all-start.1) | async-done | bytes 524320 | tf_op jit(solution)/shard_map/all_to_all | solution.py:158
  130.7 5.0 all-to-all-start.3
  136.8 7.5 %fusion.78 = (bf16[2048,64]{1,0:T(8,128)(2,1)S(1)}, bf16[2048,64]{1,0:T(8,128)(2,1)S(1)}, bf16[2048,64]{1,0:T(8,128)(2,1)S(1)}, bf16[2048,64]{1,0:T(8,128)(2,1)S(1)}) fusion(f32[2048,128]{1,0:T(8,128)} %bitcast_convert_fusion, f32[64]{0:T(128)S(1)} %multiply_power_fusion, f32[2048]{0:T(1024)S(1)} %add_convert_fusion.1, f32[2048,128]{1,0:T(8,128)S(1)} %bitcast_convert_fusion.1), kind=kLoop, calls=%fused_computation.126 | loop fusion | flops 2228224 | bytes 3154176 | tf_op jit(solution)/shard_map/convert.7
  155.2 7.5 %fusion.19 = f32[512,128]{1,0:T(8,128)} fusion(f32[512,6144]{1,0:T(8,128)} %copy-done.2, f32[512]{0:T(512)S(1)} %max.37, bf16[2048,128]{1,0:T(8,128)(2,1)S(1)} %bitcast.182, bf16[4096,128]{1,0:T(8,128)(2,1)} %get-tuple-element.44), kind=kOutput, calls=%fused_computation.43 | convolution fusion | flops 814743552 | bytes 14419968 | tf_op jit(solution)/shard_map/while/body/eval_jaxpr/dot_general | solution.py:78
  171.1 8.4 %fusion.143 = (f32[512]{0:T(512)S(1)}, f32[512,6144]{1,0:T(8,128)S(1)}) fusion(bf16[512,128]{1,0:T(8,128)(2,1)S(1)} %copy-done.21, bf16[2048,64]{1,0:T(8,128)(2,1)} %copy-done.12, bf16[2048,64]{1,0:T(8,128)(2,1)S(1)} %copy-done.11, bf16[4096,128]{1,0:T(8,128)(2,1)} %get-tuple-element.45, pred[512,2048]{1,0:T(32,128)(4,1)} %iota_compare_fusion.6, ...), kind=kOutput, calls=%fused_computation.234 | convolution fusion | flops 822607360 | bytes 17434624 | tf_op jit(solution)/shard_map/while/body/eval_jaxpr/qd,kd->qk/dot_general | solution.py:62
  181.6 8.6 %fusion.145 = (f32[512]{0:T(512)S(1)}, f32[512,6144]{1,0:T(8,128)}) fusion(bf16[512,128]{1,0:T(8,128)(2,1)S(1)} %copy-done.20, bf16[2048,64]{1,0:T(8,128)(2,1)} %copy-done.12, bf16[2048,64]{1,0:T(8,128)(2,1)S(1)} %copy-done.11, bf16[4096,128]{1,0:T(8,128)(2,1)} %get-tuple-element.45, pred[512,2048]{1,0:T(32,128)(4,1)} %iota_compare_fusion.7, ...), kind=kOutput, calls=%fused_computation.236 | convolution fusion | flops 822607360 | bytes 17434624 | tf_op jit(solution)/shard_map/while/body/eval_jaxpr/qd,kd->qk/dot_general | solution.py:62
  190.3 6.4 fusion.1
  204.2 8.9 %copy.87 = bf16[1,2048,128]{2,0,1:T(2,128)(2,1)} copy(bf16[1,2048,128]{2,1,0:T(8,128)(2,1)S(1)} %maximum_bitcast_fusion) | data formatting | bytes 1048576 | tf_op jit(solution)/shard_map/while/body/jit(dynamic_update_index_in_dim)/broadcast_in_dim | solution.py:183
  213.7 13.7 %reduce = bf16[2048,128]{1,0:T(8,128)(2,1)} reduce(bf16[2048,1,128]{2,1,0:T(2,128)(2,1)} %bitcast.190, bf16[]{:T(256)} %broadcast.488), dimensions={1}, to_apply=%bitcast.179.reduce_sub_computation | reduce | bytes 1048578
  229.3 7.5 %all-to-all-start.4 = ((bf16[32,2,4096]{2,1,0:T(2,128)(2,1)}), bf16[32,2,4096]{2,1,0:T(2,128)(2,1)}, u32[]{:S(2)}, u32[]{:S(2)}) async-start(bf16[32,2,4096]{2,1,0:T(2,128)(2,1)} %reshape.401), calls=%async_computation.4 | async-start | bytes 1048576 | tf_op jit(solution)/shard_map/all_to_all | solution.py:189
  239.5 6.6 gather_fusion.4
  255.5 5.0 multiply_reduce_fusion.1
  265.1 6.3 reshape.379
  273.9 143.6 %scatter_fusion = bf16[64,2,8,2048]{3,2,1,0:T(8,128)(2,1)} fusion(bf16[64,2,8,2048]{3,2,1,0:T(8,128)(2,1)} %broadcast_in_dim.180, s32[768]{0:T(1024)S(1)} %reshape.377, bf16[768,2048]{1,0:T(8,128)(2,1)} %reshape.379), kind=kCustom, calls=%fused_computation.8 | custom fusion | bytes 9446400 | tf_op jit(solution)/shard_map/scatter | solution.py:215
  417.5 6.8 broadcast_in_dim.183
  424.2 106.8 %all_to_all.54 = bf16[128,1,2,8,2048]{4,3,2,1,0:T(8,128)(2,1)S(1)} all-to-all(bf16[128,1,2,8,2048]{4,3,2,1,0:T(8,128)(2,1)} %bitcast.181), channel_id=1, replica_groups=mesh['req'=4,'exp'=32] {'req','exp'}, dimensions={0} | all-to-all | bytes 16777216 | tf_op jit(solution)/shard_map/all_to_all | solution.py:226
  534.3 12.8 %fusion.9 = f32[128,2,8,704]{0,3,2,1:T(8,128)} fusion(bf16[128,1,2,8,2048]{4,3,2,1,0:T(8,128)(2,1)S(1)} %all_to_all.54, bf16[2048,704]{0,1:T(8,128)(2,1)S(1)} %copy-done.36), kind=kOutput, calls=%fused_computation.27 | convolution fusion | flops 5905580032 | bytes 17039360 | tf_op jit(solution)/shard_map/nsrkd,dsf->nsrkf/dot_general | solution.py:230
  547.1 27.3 %convert_bitcast_fusion = bf16[128,1,2,8,2048]{4,0,3,2,1:T(8,128)(2,1)} fusion(bf16[704,2048]{1,0:T(8,128)(2,1)S(1)} %copy-done, f32[128,2,8,704]{0,3,2,1:T(8,128)} %fusion.9, bf16[128,1,2,8,2048]{4,3,2,1,0:T(8,128)(2,1)} %copy-done.7, bf16[2048,704]{0,1:T(8,128)(2,1)} %param.31), kind=kOutput, calls=%fused_computation.32 | convolution fusion | flops 11824005120 | bytes 28311552 | tf_op jit(solution)/shard_map/nsrkf,sfd->nsrkd/dot_general | solution.py:233
  574.4 11.2 %copy.62 = bf16[128,1,2,8,2048]{4,3,2,1,0:T(8,128)(2,1)} copy(bf16[128,1,2,8,2048]{4,0,3,2,1:T(8,128)(2,1)} %convert_bitcast_fusion) | data formatting | bytes 16777216 | tf_op jit(solution)/shard_map/convert_element_type | solution.py:235
  585.7 6.2 all-to-all-start.6
  594.5 8.7 %fusion.44 = bf16[1,2,4096,128]{3,2,1,0:T(8,128)(2,1)} fusion(s32[]{:T(128)S(6)} %select_n.213, bf16[2,2048,128]{2,1,0:T(8,128)(2,1)} %slice.118, bf16[1,2048,64]{2,1,0:T(8,128)(2,1)} %bitcast.192, bf16[1,2048,64]{2,1,0:T(8,128)(2,1)} %bitcast.193, bf16[1,2048,128]{2,1,0:T(8,128)(2,1)S(1)} %bitcast.186), kind=kLoop, calls=%fused_computation.80 | loop fusion | flops 16777216 | bytes 4194308 | tf_op jit(solution)/shard_map/while/body/jit(dynamic_update_index_in_dim)/broadcast_in_dim | solution.py:183
  603.5 6.6 gather_fusion.3
  610.5 85.9 %all-to-all-done.6 = bf16[128,1,2,8,2048]{4,3,2,1,0:T(8,128)(2,1)} async-done(((bf16[128,1,2,8,2048]{4,3,2,1,0:T(8,128)(2,1)}), bf16[128,1,2,8,2048]{4,3,2,1,0:T(8,128)(2,1)}, u32[]{:S(2)}, u32[]{:S(2)}) %all-to-all-start.6) | async-done | bytes 8388640 | tf_op jit(solution)/shard_map/all_to_all | solution.py:232
  696.4 9.6 %convert_reduce_fusion = f32[64,2,8,2048]{3,2,1,0:T(8,128)} fusion(bf16[64,2,2,8,2048]{4,3,2,1,0:T(8,128)(2,1)} %bitcast.180), kind=kLoop, calls=%fused_computation.10 | loop fusion | flops 6291456 | bytes 16777216 | tf_op jit(solution)/shard_map/reduce_sum | solution.py:244
  706.0 15.5 %gather_fusion.2 = f32[768,2048]{1,0:T(8,128)} fusion(f32[64,2,8,2048]{3,2,1,0:T(8,128)} %convert_reduce_fusion, s32[768]{0:T(1024)S(1)} %reshape.359), kind=kCustom, calls=%fused_computation.5 | custom fusion | bytes 12592128 | tf_op jit(solution)/shard_map/gather | solution.py:245
  721.5 8.1 %reshape.362 = f32[2,64,6,2048]{3,2,1,0:T(8,128)} reshape(f32[768,2048]{1,0:T(8,128)} %gather_fusion.2) | data formatting | bytes 12582912 | tf_op jit(solution)/shard_map/gather | solution.py:245
  729.6 6.7 multiply_reduce_fusion
  (176 shorter events, 97.5 us)
Async XLA Ops:
  7.2 539.9 %copy-start = (bf16[704,2048]{1,0:T(8,128)(2,1)S(1)}, bf16[704,2048]{1,0:T(8,128)(2,1)}, u32[]{:S(2)}) copy-start(bf16[704,2048]{1,0:T(8,128)(2,1)} %param.33) | copy-start | bytes 8650756
  7.2 10.1 %copy-start.37 = (s32[8]{0:T(128)S(1)}, s32[8]{0:T(128)}, u32[]{:S(2)}) copy-start(s32[8]{0:T(128)} %param.25) | copy-start | bytes 100
  7.2 77.9 %all-gather.8.cloned.1.call-start = ((), (), s32[]{:S(2)}) async-start(), calls=%async_computation.9 | async-start | bytes 2621440 | tf_op jit(solution)/shard_map/all_gather | solution.py:149
  7.9 83.1 %all-gather.6.cloned.1.call-start = ((), (), s32[]{:S(2)}) async-start(), calls=%async_computation.8 | async-start | bytes 2621440 | tf_op jit(solution)/shard_map/all_gather | solution.py:148
  8.7 11.2 %copy-start.35 = (s32[8]{0:T(128)S(1)}, s32[8]{0:T(128)}, u32[]{:S(2)}) copy-start(s32[8]{0:T(128)} %param.24) | copy-start | bytes 100
  8.7 11.2 %copy-start.34 = (s32[2,64,6]{1,0,2:T(2,128)S(1)}, s32[2,64,6]{1,0,2:T(2,128)}, u32[]{:S(2)}) copy-start(s32[2,64,6]{1,0,2:T(2,128)} %param.23) | copy-start | bytes 9220
  11.6 71.2 %all-to-all-start = ((bf16[8,16,64,128]{3,2,1,0:T(8,128)(2,1)}), bf16[8,16,64,128]{3,2,1,0:T(8,128)(2,1)}, u32[]{:S(2)}, u32[]{:S(2)}) async-start(bf16[8,16,64,128]{3,2,1,0:T(8,128)(2,1)} %bitcast.188), calls=%async_computation | async-start | bytes 4194304 | tf_op jit(solution)/shard_map/all_to_all | solution.py:12
  16.5 230.1 %all-gather.4.cloned.1.call-start = ((), (), s32[]{:S(2)}) async-start(), calls=%async_computation.7 | async-start | bytes 2621440 | tf_op jit(solution)/shard_map/all_gather | solution.py:146
  19.9 74.1 %copy-start.29 = (pred[2]{0:T(512)(128)(4,1)}, pred[2]{0:T(512)(128)(4,1)S(1)}, u32[]{:S(2)}) copy-start(pred[2]{0:T(512)(128)(4,1)S(1)} %get-tuple-element.42) | copy-start | bytes 10
  19.9 71.1 %copy-start.31 = (s32[1024]{0:T(1024)}, s32[1024]{0:T(1024)S(1)}, u32[]{:S(2)}) copy-start(s32[1024]{0:T(1024)S(1)} %pad_clamp_fusion) | copy-start | bytes 12292
  64.5 172.4 %copy-start.27 = (s32[2,64,6]{1,2,0:T(8,128)}, s32[2,64,6]{1,2,0:T(8,128)S(1)}, u32[]{:S(2)}) copy-start(s32[2,64,6]{1,2,0:T(8,128)S(1)} %broadcast_select_fusion.3) | copy-start | bytes 9220
  96.5 17.9 %all-to-all-start.2 = ((bf16[32,64,128]{2,1,0:T(8,128)(2,1)}), bf16[32,64,128]{2,1,0:T(8,128)(2,1)S(1)}, u32[]{:S(2)}, u32[]{:S(2)}) async-start(bf16[32,64,128]{2,1,0:T(8,128)(2,1)} %bitcast.197), calls=%async_computation.2 | async-start | bytes 1048576 | tf_op jit(solution)/shard_map/all_to_all | solution.py:165
  114.5 16.2 %all-to-all-start.1 = ((bf16[32,64,128]{2,1,0:T(8,128)(2,1)}), bf16[32,64,128]{2,1,0:T(8,128)(2,1)}, u32[]{:S(2)}, u32[]{:S(2)}) async-start(bf16[32,64,128]{2,1,0:T(8,128)(2,1)} %bitcast.196), calls=%async_computation.1 | async-start | bytes 1048576 | tf_op jit(solution)/shard_map/all_to_all | solution.py:158
  130.7 24.5 %all-to-all-start.3 = ((bf16[32,64,128]{2,1,0:T(8,128)(2,1)}), bf16[32,64,128]{2,1,0:T(8,128)(2,1)S(1)}, u32[]{:S(2)}, u32[]{:S(2)}) async-start(bf16[32,64,128]{2,1,0:T(8,128)(2,1)} %bitcast.195), calls=%async_computation.3 | async-start | bytes 1048576 | tf_op jit(solution)/shard_map/all_to_all | solution.py:172
  136.8 8.7 %copy-start.33 = (bf16[1,2,4,128]{3,2,1,0:T(4,128)(2,1)S(1)}, bf16[1,2,4,128]{3,2,1,0:T(4,128)(2,1)}, u32[]{:S(2)}) copy-start(bf16[1,2,4,128]{3,2,1,0:T(4,128)(2,1)} %param.27) | copy-start | bytes 6148
  136.8 8.8 %copy-start.15 = (pred[512,4096]{1,0:T(32,128)(4,1)S(1)}, pred[512,4096]{1,0:T(32,128)(4,1)}, u32[]{:S(2)}) copy-start(pred[512,4096]{1,0:T(32,128)(4,1)} %get-tuple-element.61) | copy-start | bytes 6291460
  136.8 8.8 %copy-start.17 = (pred[512,2048]{1,0:T(32,128)(4,1)S(1)}, pred[512,2048]{1,0:T(32,128)(4,1)}, u32[]{:S(2)}) copy-start(pred[512,2048]{1,0:T(32,128)(4,1)} %iota_compare_fusion.4) | copy-start | bytes 3145732
  136.8 8.8 %copy-start.18 = (bf16[4096,128]{1,0:T(8,128)(2,1)S(1)}, bf16[4096,128]{1,0:T(8,128)(2,1)}, u32[]{:S(2)}) copy-start(bf16[4096,128]{1,0:T(8,128)(2,1)} %get-tuple-element.45) | copy-start | bytes 3145732
  155.1 7.6 %copy-start.22 = (bf16[512,128]{1,0:T(8,128)(2,1)S(1)}, bf16[512,128]{1,0:T(8,128)(2,1)}, u32[]{:S(2)}) copy-start(bf16[512,128]{1,0:T(8,128)(2,1)} %get-tuple-element.53) | copy-start | bytes 393220
  155.1 7.7 %copy-start.11 = (bf16[2048,64]{1,0:T(8,128)(2,1)S(1)}, bf16[2048,64]{1,0:T(8,128)(2,1)}, u32[]{:S(2)}) copy-start(bf16[2048,64]{1,0:T(8,128)(2,1)} %copy-done.10) | copy-start | bytes 786436
  155.2 7.7 %copy-start.13 = (bf16[2048,64]{1,0:T(8,128)(2,1)S(1)}, bf16[2048,64]{1,0:T(8,128)(2,1)}, u32[]{:S(2)}) copy-start(bf16[2048,64]{1,0:T(8,128)(2,1)} %copy-done.12) | copy-start | bytes 786436
  155.2 7.7 %copy-start.14 = (pred[512,4096]{1,0:T(32,128)(4,1)S(1)}, pred[512,4096]{1,0:T(32,128)(4,1)}, u32[]{:S(2)}) copy-start(pred[512,4096]{1,0:T(32,128)(4,1)} %get-tuple-element.60) | copy-start | bytes 6291460
  155.2 7.7 %copy-start.16 = (pred[512,2048]{1,0:T(32,128)(4,1)S(1)}, pred[512,2048]{1,0:T(32,128)(4,1)}, u32[]{:S(2)}) copy-start(pred[512,2048]{1,0:T(32,128)(4,1)} %iota_compare_fusion.5) | copy-start | bytes 3145732
  155.2 7.7 %copy-start.19 = (bf16[4096,128]{1,0:T(8,128)(2,1)S(1)}, bf16[4096,128]{1,0:T(8,128)(2,1)}, u32[]{:S(2)}) copy-start(bf16[4096,128]{1,0:T(8,128)(2,1)} %get-tuple-element.45) | copy-start | bytes 3145732
  190.3 6.8 copy-start.24
  229.3 20.4 %all-to-all-start.4 = ((bf16[32,2,4096]{2,1,0:T(2,128)(2,1)}), bf16[32,2,4096]{2,1,0:T(2,128)(2,1)}, u32[]{:S(2)}, u32[]{:S(2)}) async-start(bf16[32,2,4096]{2,1,0:T(2,128)(2,1)} %reshape.401), calls=%async_computation.4 | async-start | bytes 1048576 | tf_op jit(solution)/shard_map/all_to_all | solution.py:189
  239.5 6.8 copy-start.30
  424.2 110.0 %copy-start.36 = (bf16[2048,704]{0,1:T(8,128)(2,1)S(1)}, bf16[2048,704]{0,1:T(8,128)(2,1)}, u32[]{:S(2)}) copy-start(bf16[2048,704]{0,1:T(8,128)(2,1)} %param.32) | copy-start | bytes 8650756
  585.7 110.8 %all-to-all-start.6 = ((bf16[128,1,2,8,2048]{4,3,2,1,0:T(8,128)(2,1)}), bf16[128,1,2,8,2048]{4,3,2,1,0:T(8,128)(2,1)}, u32[]{:S(2)}, u32[]{:S(2)}) async-start(bf16[128,1,2,8,2048]{4,3,2,1,0:T(8,128)(2,1)} %copy.62), calls=%async_computation.6 | async-start | bytes 16777216 | tf_op jit(solution)/shard_map/all_to_all | solution.py:232
  594.5 8.7 %copy-start.9 = (bf16[2,64,2048]{2,1,0:T(8,128)(2,1)S(1)}, bf16[2,64,2048]{2,1,0:T(8,128)(2,1)}, u32[]{:S(2)}) copy-start(bf16[2,64,2048]{2,1,0:T(8,128)(2,1)} %copy-done.8) | copy-start | bytes 1572868
  594.5 8.7 %copy-start.25 = (bf16[2048,64]{0,1:T(8,128)(2,1)S(1)}, bf16[2048,64]{0,1:T(8,128)(2,1)}, u32[]{:S(2)}) copy-start(bf16[2048,64]{0,1:T(8,128)(2,1)} %param.30) | copy-start | bytes 786436
  603.5 6.8 copy-start.28
  (15 other events, 51.4 us)
Sparse Core Ops, SparseCore 0:
  9.7 47.9 all-gather.7
  59.3 31.7 all-gather.5
  92.7 30.7 all-gather.3
